TPU v7x, 128 devices: a whole 4x4x4 slice. The times are simulated.
128 devices in a mesh: query: 4 (over z_lo, core), lib: 32 (over x, y, z_hi).
Axes of the slice: x: 4, y: 4, z: 4 (z_hi: 2, z_lo: 2; z = z_hi * 2 + z_lo), core: 2. Of those that a mesh axis runs over, the one named last changes fastest.
Arguments:
- queries: bfloat16 [4096, 2048], P(('query', 'lib')), may hold values from -64 to 64
- query_bucket: int32 [4096], P(('query', 'lib')), may hold values from 0 to 63, as said below
- library: bfloat16 [98304, 2048], P(('lib', 'query')), may hold values from -64 to 64
- library_time: bfloat16 [98304], P(('lib', 'query')), may hold values from 0 to 2
- library_bucket: int32 [98304], P(('lib', 'query')), may hold values from 0 to 63, as said below
Outputs:
- expected_spectra: bfloat16 [4096, 2048], P(('query', 'lib'))
- expected_time: float32 [4096], P(('query', 'lib'))
- log_evidence: float32 [4096], P(('query', 'lib'))
Inputs may be any that keep to these rules, and one draw needn't show every extreme that they name: `query_bucket`: library entries whose bucket differs from a query's by at most one are that query's candidates; the queries held by the devices at index i of lib lie in buckets 2 i and 2 i + 1. `library_bucket`: the library entries of every device hold each of the 64 buckets exactly 3072 // 256 times.
All inputs are finite; a program needn't handle non-finite values.
Results may differ from a plain program's by a relative error of at most 0.003.
Values may be sent and summed in bfloat16 or wider, within the bound.
A program may use at most 128 MiB of HBM per device.

v0:
```python
import jax
import jax.numpy as jnp
from jax import lax
from jax.sharding import PartitionSpec as P

SHARPNESS = 448


def entry_scale(spectra_rows):
    return lax.rsqrt(jnp.mean(jnp.square(spectra_rows.astype(jnp.float32)), axis=1) + 1e-06)


def scaled_scores(query_block, query_scale, block_bucket, entries, entry_bucket):
    products = lax.dot_general(
        query_block, entries, (((1,), (1,)), ((), ())), preferred_element_type=jnp.float32
    )
    inside = jnp.abs(block_bucket[:, None] - entry_bucket[None, :]) <= 1
    return jnp.where(
        inside, products * query_scale[:, None] * entry_scale(entries)[None, :], -jnp.inf
    )


def finish(spectra_sum, totals, time_sum, own_maxima):
    expected = (spectra_sum / totals[:, None]).astype(jnp.bfloat16)
    return (expected, time_sum / totals, own_maxima + jnp.log(totals))


def per_device(queries, query_bucket, library, library_time, library_bucket):
    own_rows = queries.shape[0]
    bin_count = queries.shape[1]
    query_block, block_bucket = (
        lax.all_gather(queries, "lib", axis=0, tiled=True),
        lax.all_gather(query_bucket, "lib", axis=0, tiled=True),
    )
    query_scale = entry_scale(query_block) * (SHARPNESS / bin_count)
    entries, entry_time, entry_bucket = (
        lax.all_gather(library, "query", axis=0, tiled=True),
        lax.all_gather(library_time, "query", axis=0, tiled=True),
        lax.all_gather(library_bucket, "query", axis=0, tiled=True),
    )
    scores = scaled_scores(query_block, query_scale, block_bucket, entries, entry_bucket)
    maxima = lax.pmax(jnp.max(scores, axis=1), "lib")
    weights = jnp.exp(scores - maxima[:, None]).astype(jnp.bfloat16)
    total_part = jnp.sum(weights.astype(jnp.float32), axis=1)
    spectra_part = jnp.dot(weights, entries, preferred_element_type=jnp.float32)
    time_part = jnp.dot(weights, entry_time, preferred_element_type=jnp.float32)
    first_row = lax.axis_index("lib") * own_rows
    total_all, time_all = lax.psum((total_part, time_part), "lib")
    spectra_sum = lax.psum_scatter(spectra_part, "lib", scatter_dimension=0, tiled=True)
    totals = lax.dynamic_slice_in_dim(total_all, first_row, own_rows)
    time_sum = lax.dynamic_slice_in_dim(time_all, first_row, own_rows)
    own_maxima = lax.dynamic_slice_in_dim(maxima, first_row, own_rows)
    return finish(spectra_sum, totals, time_sum, own_maxima)


def solution(mesh):
    placed = (
        P(("query", "lib"), None),
        P(("query", "lib")),
        P(("lib", "query"), None),
        P(("lib", "query")),
        P(("lib", "query")),
    )
    return jax.shard_map(
        per_device,
        mesh=mesh,
        in_specs=placed,
        out_specs=(P(("query", "lib"), None), P(("query", "lib")), P(("query", "lib"))),
        check_vma=False,
    )
```

profile of v0, /device:TPU:0, one launch (start us, length us, event | category | flops | bytes accessed | tf_op | source)
XLA Modules:
  0.0 572.3 jit_solution(1006789328680344113)
XLA Ops:
  7.2 0.7 all-gather.5.cloned.1.call-update
  7.9 0.7 all-gather.7.cloned.1.call-update
  8.6 0.0 reduce-scatter.2.cloned.1.call-start
  8.7 0.7 reshape.24
  9.4 1.2 dynamic-slice
  11.3 0.9 dynamic-update-slice
  12.2 21.3 %all-reduce = s32[1024]{0:T(1024)S(1)} all-reduce(s32[1024]{0:T(1024)S(1)} %dynamic-update-slice), channel_id=1, replica_groups=mesh['query'=4,'lib'=32] {'lib'}, use_global_device_ids=true, to_apply=%add | all-reduce | flops 1024 | bytes 8192
  33.5 5.2 all-gather
  38.7 57.0 %all-gather.5.cloned.1.call-done = bf16[1024,2048]{1,0:T(8,128)(2,1)} async-done(((bf16[32,2048]{1,0:T(8,128)(2,1)}), bf16[1024,2048]{1,0:T(8,128)(2,1)}) %all-gather.5.cloned.1.call-update) | async-done | bytes 4194320 | tf_op jit(solution)/shard_map/all_gather | solution.py:32
  95.7 3.1 multiply_reduce_fusion.1
  98.8 109.7 %all-gather.7.cloned.1.call-done = bf16[3072,2048]{1,0:T(8,128)(2,1)} async-done(((bf16[768,2048]{1,0:T(8,128)(2,1)}), bf16[3072,2048]{1,0:T(8,128)(2,1)}) %all-gather.7.cloned.1.call-update) | async-done | bytes 12582928 | tf_op jit(solution)/shard_map/all_gather | solution.py:37
  208.4 7.2 %multiply_reduce_fusion = f32[3072]{0:T(1024)S(1)} fusion(bf16[3072,2048]{1,0:T(8,128)(2,1)} %all-gather.7.cloned.1.call-done), kind=kLoop, calls=%fused_computation | loop fusion | flops 18871296 | bytes 12595200 | tf_op jit(solution)/shard_map/reduce_sum | solution.py:10
  215.7 19.3 %fusion = (f32[1024]{0:T(1024)S(1)}, f32[1024,3072]{1,0:T(8,128)}) fusion(f32[3072]{0:T(1024)S(1)} %add_rsqrt_fusion, f32[1024]{0:T(1024)S(1)} %rsqrt_multiply_fusion, s32[3072]{0:T(1024)S(1)} %bitcast.10, s32[1024]{0:T(1024)S(1)} %all-reduce, bf16[1024,2048]{1,0:T(8,128)(2,1)S(1)} %copy-done.1, bf16[3072,2048]{1,0:T(8,128)(2,1)} %all-gather.7.cloned.1.call-done), kind=kOutput, calls=%fused_computation.6 | convolution fusion | flops 12906920960 | bytes 29396992 | tf_op jit(solution)/shard_map/dot_general | solution.py:14
  235.0 96.7 %pmax.7 = f32[1024]{0:T(1024)S(1)} all-reduce(f32[1024]{0:T(1024)S(1)} %get-tuple-element.9), channel_id=1, replica_groups=mesh['query'=4,'lib'=32] {'lib'}, use_global_device_ids=true, to_apply=%region_3.4 | all-reduce | flops 1024 | bytes 8192 | tf_op jit(solution)/shard_map/pmax | solution.py:42
  331.7 8.3 %convert_reduce_fusion = (f32[1024]{0:T(1024)S(1)}, bf16[1024,3072]{1,0:T(8,128)(2,1)S(1)}) fusion(f32[1024]{0:T(1024)S(1)} %pmax.7, f32[3072]{0:T(1024)S(1)} %add_rsqrt_fusion, f32[1024,3072]{1,0:T(8,128)} %get-tuple-element.10, f32[1024]{0:T(1024)S(1)} %rsqrt_multiply_fusion, s32[3072]{0:T(1024)S(1)} %bitcast.11, s32[1024]{0:T(1024)S(1)} %all-reduce), kind=kLoop, calls=%fused_computation.1 | loop fusion | flops 31456256 | bytes 18915328 | tf_op jit(solution)/shard_map/reduce_sum | solution.py:44
  340.0 2.7 copy-done
  342.6 16.9 %fusion.1 = f32[1024,2048]{1,0:T(8,128)} fusion(bf16[1024,3072]{1,0:T(8,128)(2,1)S(1)} %get-tuple-element.8, bf16[3072,2048]{1,0:T(8,128)(2,1)} %all-gather.7.cloned.1.call-done), kind=kOutput, calls=%fused_computation.12 | convolution fusion | flops 12884901888 | bytes 27262976 | tf_op jit(solution)/shard_map/dot_general | solution.py:45
  359.6 5.2 all-gather.1
  364.8 4.5 fusion.2
  369.3 90.5 %all-reduce.1 = (f32[1024]{0:T(1024)S(1)}, f32[1024]{0:T(1024)S(1)}) all-reduce(f32[1024]{0:T(1024)S(1)} %get-tuple-element.7, f32[1024]{0:T(1024)S(1)} %bitcast.13), channel_id=1, replica_groups=mesh['query'=4,'lib'=32] {'lib'}, use_global_device_ids=true, to_apply=%region_6.7 | all-reduce | flops 2048 | bytes 16384 | tf_op jit(solution)/shard_map/psum | solution.py:48
  459.8 0.6 log_add_fusion
  460.4 0.6 dynamic-slice_divide_fusion
  461.0 103.1 %reduce-scatter.2.cloned.1.call-done = f32[32,2048]{1,0:T(8,128)} async-done(((f32[1024,2048]{1,0:T(8,128)}), f32[32,2048]{1,0:T(8,128)}) %reduce-scatter.2.cloned.1.call-update) | async-done | bytes 262160 | tf_op jit(solution)/shard_map/reduce_scatter | solution.py:49
  564.1 1.7 divide_convert_fusion
  (12 shorter events, 0.1 us)
Async XLA Ops:
  7.2 88.5 %all-gather.5.cloned.1.call-start = ((), (), s32[]{:S(2)}) async-start(), calls=%async_computation.1 | async-start | bytes 4325376 | tf_op jit(solution)/shard_map/all_gather | solution.py:32
  7.9 200.5 %all-gather.7.cloned.1.call-start = ((), (), s32[]{:S(2)}) async-start(), calls=%async_computation.2 | async-start | bytes 15728640 | tf_op jit(solution)/shard_map/all_gather | solution.py:37
  8.6 555.5 %reduce-scatter.2.cloned.1.call-start = ((), (), s32[]{:S(2)}) async-start(), calls=%async_computation.3 | async-start | bytes 8650752 | tf_op jit(solution)/shard_map/reduce_scatter | solution.py:49
  208.4 7.3 %copy-start.1 = (bf16[1024,2048]{1,0:T(8,128)(2,1)S(1)}, bf16[1024,2048]{1,0:T(8,128)(2,1)}, u32[]{:S(2)}) copy-start(bf16[1024,2048]{1,0:T(8,128)(2,1)} %all-gather.5.cloned.1.call-done) | copy-start | bytes 12582916
  339.9 2.7 copy-start
  342.6 17.0 %copy-start.2 = (bf16[768]{0:T(1024)(128)(2,1)S(1)}, bf16[768]{0:T(1024)(128)(2,1)}, u32[]{:S(2)}) copy-start(bf16[768]{0:T(1024)(128)(2,1)} %param.8) | copy-start | bytes 4612
Sparse Core Ops, SparseCore 0:
  11.0 84.6 all-gather.4
  97.4 111.0 all-gather.6
  359.7 204.3 reduce-scatter.1
where the time goes:
time: 573 us; the launch traced here: 572 us
  waiting for transfers between devices  271 us (47%)
  blocking collectives  219 us (38%)
  matrix products  40.7 us (7%)
  other arithmetic  21.5 us (4%)
  between operations  14.5 us (3%)
    all_gather x1, waiting for transfers between devices, per_device(): lax.all_gather(library, 'query', axis=0, tiled=True)  110 us
    reduce_scatter x1, waiting for transfers between devices, per_device(): lax.psum_scatter(spectra_part, 'lib', scatter_dimension=0, tiled=True)  103 us
    pmax x1, blocking collectives, per_device(): maxima = lax.pmax(jnp.max(scores, axis=1), 'lib')  96.7 us
    psum x1, blocking collectives, per_device(): total_all, time_all = lax.psum((total_part, time_part), 'lib')  90.5 us
    all_gather x1, waiting for transfers between devices, per_device(): lax.all_gather(queries, 'lib', axis=0, tiled=True)  57 us
    unnamed x1, blocking collectives  21.3 us
    dot_general x1, matrix products, scaled_scores(): lax.dot_general(query_block, entries, (((1,), (1,)), ((), ())), preferred...  19.3 us
    dot_general x1, matrix products, per_device(): spectra_part = jnp.dot(weights, entries, preferred_element_type=jnp.float32)  16.9 us
  transfers between devices with their start and end apart: 3, of which 3 were waited for; matrix products, arithmetic and copies ran while one was open for 2% of the time, Pallas kernels for 0%

commit v1 on v0

--- a/solution.py
+++ b/solution.py
@@ -29,7 +29,9 @@
     own_rows = queries.shape[0]
     bin_count = queries.shape[1]
     query_block, block_bucket = (
-        lax.all_gather(queries, "lib", axis=0, tiled=True),
+        jnp.concatenate(
+            lax.all_to_all(jnp.stack([queries] * lax.axis_size("lib")), "lib", 0, 0), axis=0
+        ),
         lax.all_gather(query_bucket, "lib", axis=0, tiled=True),
     )
     query_scale = entry_scale(query_block) * (SHARPNESS / bin_count)

time: 573 us -> 535 us (0.934)
  waiting for transfers between devices: 271 us -> 178 us
  blocking collectives: 219 us -> 262 us
  starting transfers between devices: 0.11 us -> 11 us
    all_gather x1 -> x0, waiting for transfers between devices: 57 us -> none  [per_device(): lax.all_gather(queries, 'lib', axis=0, tiled=True)]
    unnamed x1, blocking collectives: 21.3 us -> 63.3 us
    all_gather x1, waiting for transfers between devices: 110 us -> 74.4 us  [per_device(): lax.all_gather(library, 'query', axis=0, tiled=True)]
    all_to_all x0 -> x1, starting transfers between devices: none -> 10.9 us  [per_device(): lax.all_to_all(jnp.stack([queries] * lax.axis_size('lib')), 'lib', 0, 0)]
  transfers between devices with their start and end apart: 3 -> 3, of which waited for: 3 -> 2; matrix products, arithmetic and copies ran while one was open for 2% -> 2% of each run, Pallas kernels for 0% -> 0%
where the time goes in v1:
time: 535 us
  blocking collectives  262 us (49%)
  waiting for transfers between devices  178 us (33%)
  matrix products  41.6 us (8%)
  other arithmetic  21.2 us (4%)
  between operations  14.9 us (3%)
  starting transfers between devices  11 us (2%)
  local copies, waits for them, and re-layouts  6.98 us (1%)
    reduce_scatter x1, waiting for transfers between devices, per_device(): lax.psum_scatter(spectra_part, 'lib', scatter_dimension=0, tiled=True)  103 us
    pmax x1, blocking collectives, per_device(): maxima = lax.pmax(jnp.max(scores, axis=1), 'lib')  96.9 us
    psum x1, blocking collectives, per_device(): total_all, time_all = lax.psum((total_part, time_part), 'lib')  91 us
    all_gather x1, waiting for transfers between devices, per_device(): lax.all_gather(library, 'query', axis=0, tiled=True)  74.4 us
    unnamed x1, blocking collectives  63.3 us
    dot_general x1, matrix products, scaled_scores(): lax.dot_general(query_block, entries, (((1,), (1,)), ((), ())), preferred...  20.2 us
    dot_general x1, matrix products, per_device(): spectra_part = jnp.dot(weights, entries, preferred_element_type=jnp.float32)  16.9 us
    all_to_all x1, starting transfers between devices, per_device(): lax.all_to_all(jnp.stack([queries] * lax.axis_size('lib')), 'lib', 0, 0)  10.9 us
  transfers between devices with their start and end apart: 3, of which 2 were waited for; matrix products, arithmetic and copies ran while one was open for 2% of the time, Pallas kernels for 0%

profile of v1, /device:TPU:0, one launch (start us, length us, event | category | flops | bytes accessed | tf_op | source)
XLA Modules:
  0.0 534.9 jit_solution(1883145540416498683)
XLA Ops:
  7.2 0.7 all-gather.4.cloned.1.call-update
  7.9 3.4 stack.2
  11.3 10.9 %all-to-all-start = ((bf16[32,32,2048]{2,1,0:T(8,128)(2,1)}), bf16[32,32,2048]{2,1,0:T(8,128)(2,1)}, u32[]{:S(2)}, u32[]{:S(2)}) async-start(bf16[32,32,2048]{2,1,0:T(8,128)(2,1)} %stack.2), calls=%async_computation | async-start | bytes 8388608 | tf_op jit(solution)/shard_map/all_to_all | solution.py:33
  22.2 0.0 reduce-scatter.2.cloned.1.call-start
  22.3 0.6 dynamic-slice
  23.6 0.2 dynamic-update-slice
  23.8 63.3 %all-reduce = s32[1024]{0:T(1024)S(1)} all-reduce(s32[1024]{0:T(1024)S(1)} %dynamic-update-slice), channel_id=1, replica_groups=mesh['query'=4,'lib'=32] {'lib'}, use_global_device_ids=true, to_apply=%add | all-reduce | flops 1024 | bytes 8192
  87.1 5.4 %all-gather = s32[4,1,768]{2,1,0:T(1,128)S(1)} all-gather(s32[1,1,768]{2,1,0:T(1,128)S(1)} %reshape.41), channel_id=1, replica_groups=mesh['query'=4,'lib'=32] {'query'}, dimensions={0}, use_global_device_ids=true | all-gather | bytes 15360 | tf_op jit(solution)/shard_map/all_gather | solution.py:41
  92.4 3.1 multiply_reduce_fusion.1
  95.5 0.1 mul.34
  95.6 74.4 %all-gather.4.cloned.1.call-done = bf16[3072,2048]{1,0:T(8,128)(2,1)} async-done(((bf16[768,2048]{1,0:T(8,128)(2,1)}), bf16[3072,2048]{1,0:T(8,128)(2,1)}) %all-gather.4.cloned.1.call-update) | async-done | bytes 12582928 | tf_op jit(solution)/shard_map/all_gather | solution.py:39
  170.0 7.1 %multiply_reduce_fusion = f32[3072]{0:T(1024)S(1)} fusion(bf16[3072,2048]{1,0:T(8,128)(2,1)} %all-gather.4.cloned.1.call-done), kind=kLoop, calls=%fused_computation | loop fusion | flops 18871296 | bytes 12595200 | tf_op jit(solution)/shard_map/reduce_sum | solution.py:10
  177.1 20.2 %fusion = (f32[1024]{0:T(1024)S(1)}, f32[1024,3072]{1,0:T(8,128)}) fusion(f32[3072]{0:T(1024)S(1)} %add_rsqrt_fusion, f32[1024]{0:T(1024)S(1)} %mul.34, s32[3072]{0:T(1024)S(1)} %bitcast.11, s32[1024]{0:T(1024)S(1)} %all-reduce, bf16[1024,2048]{1,0:T(8,128)(2,1)} %bitcast.2, bf16[3072,2048]{1,0:T(8,128)(2,1)} %all-gather.4.cloned.1.call-done), kind=kOutput, calls=%fused_computation.6 | convolution fusion | flops 12906920960 | bytes 29396992 | tf_op jit(solution)/shard_map/dot_general | solution.py:14
  197.3 96.9 %pmax.7 = f32[1024]{0:T(1024)S(1)} all-reduce(f32[1024]{0:T(1024)S(1)} %get-tuple-element.9), channel_id=1, replica_groups=mesh['query'=4,'lib'=32] {'lib'}, use_global_device_ids=true, to_apply=%region_3.4 | all-reduce | flops 1024 | bytes 8192 | tf_op jit(solution)/shard_map/pmax | solution.py:44
  294.2 8.2 %convert_reduce_fusion = (f32[1024]{0:T(1024)S(1)}, bf16[1024,3072]{1,0:T(8,128)(2,1)S(1)}) fusion(f32[1024]{0:T(1024)S(1)} %pmax.7, f32[3072]{0:T(1024)S(1)} %add_rsqrt_fusion, f32[1024,3072]{1,0:T(8,128)} %get-tuple-element.10, f32[1024]{0:T(1024)S(1)} %mul.34, s32[3072]{0:T(1024)S(1)} %bitcast.12, s32[1024]{0:T(1024)S(1)} %all-reduce), kind=kLoop, calls=%fused_computation.1 | loop fusion | flops 31456256 | bytes 18915328 | tf_op jit(solution)/shard_map/reduce_sum | solution.py:46
  302.4 2.7 copy-done
  305.0 16.9 %fusion.1 = f32[1024,2048]{1,0:T(8,128)} fusion(bf16[1024,3072]{1,0:T(8,128)(2,1)S(1)} %get-tuple-element.8, bf16[3072,2048]{1,0:T(8,128)(2,1)} %all-gather.4.cloned.1.call-done), kind=kOutput, calls=%fused_computation.12 | convolution fusion | flops 12884901888 | bytes 27262976 | tf_op jit(solution)/shard_map/dot_general | solution.py:47
  322.0 5.2 all-gather.1
  327.2 4.5 fusion.2
  331.7 91.0 %all-reduce.1 = (f32[1024]{0:T(1024)S(1)}, f32[1024]{0:T(1024)S(1)}) all-reduce(f32[1024]{0:T(1024)S(1)} %get-tuple-element.7, f32[1024]{0:T(1024)S(1)} %bitcast.14), channel_id=1, replica_groups=mesh['query'=4,'lib'=32] {'lib'}, use_global_device_ids=true, to_apply=%region_6.7 | all-reduce | flops 2048 | bytes 16384 | tf_op jit(solution)/shard_map/psum | solution.py:50
  422.7 0.6 log_add_fusion
  423.3 0.6 dynamic-slice_divide_fusion
  423.9 102.5 %reduce-scatter.2.cloned.1.call-done = f32[32,2048]{1,0:T(8,128)} async-done(((f32[1024,2048]{1,0:T(8,128)}), f32[32,2048]{1,0:T(8,128)}) %reduce-scatter.2.cloned.1.call-update) | async-done | bytes 262160 | tf_op jit(solution)/shard_map/reduce_scatter | solution.py:51
  526.4 1.7 divide_convert_fusion
  (17 shorter events, 0.1 us)
Async XLA Ops:
  7.2 15.1 %copy-start.4 = (u32[128]{0:T(128)S(1)}, u32[128]{0:T(128)}, u32[]{:S(2)}) copy-start(u32[128]{0:T(128)} %constant.30) | copy-start | bytes 1540
  7.2 15.1 %copy-start.1 = (s32[768]{0:T(1024)S(1)}, s32[768]{0:T(1024)}, u32[]{:S(2)}) copy-start(s32[768]{0:T(1024)} %param.9) | copy-start | bytes 9220
  7.2 16.4 %copy-start.3 = (s32[32]{0:T(128)S(1)}, s32[32]{0:T(128)}, u32[]{:S(2)}) copy-start(s32[32]{0:T(128)} %param.6) | copy-start | bytes 388
  7.2 162.8 %all-gather.4.cloned.1.call-start = ((), (), s32[]{:S(2)}) async-start(), calls=%async_computation.2 | async-start | bytes 15728640 | tf_op jit(solution)/shard_map/all_gather | solution.py:39
  11.3 81.1 %all-to-all-start = ((bf16[32,32,2048]{2,1,0:T(8,128)(2,1)}), bf16[32,32,2048]{2,1,0:T(8,128)(2,1)}, u32[]{:S(2)}, u32[]{:S(2)}) async-start(bf16[32,32,2048]{2,1,0:T(8,128)(2,1)} %stack.2), calls=%async_computation | async-start | bytes 8388608 | tf_op jit(solution)/shard_map/all_to_all | solution.py:33
  22.2 504.2 %reduce-scatter.2.cloned.1.call-start = ((), (), s32[]{:S(2)}) async-start(), calls=%async_computation.3 | async-start | bytes 8650752 | tf_op jit(solution)/shard_map/reduce_scatter | solution.py:51
  302.4 2.7 copy-start
  305.0 17.0 %copy-start.2 = (bf16[768]{0:T(1024)(128)(2,1)S(1)}, bf16[768]{0:T(1024)(128)(2,1)}, u32[]{:S(2)}) copy-start(bf16[768]{0:T(1024)(128)(2,1)} %param.8) | copy-start | bytes 4612
Sparse Core Ops, SparseCore 0:
  9.7 160.2 all-gather.3
  322.1 204.2 reduce-scatter.1
